TPU v7x, 256 devices: a whole 4x4x8 slice. The times are simulated.
256 devices in a mesh: gx: 8 (over z), gy: 32 (over x, y, core).
Axes of the slice: x: 4, y: 4, z: 8, core: 2. Of those that a mesh axis runs over, the one named last changes fastest.
Arguments:
- permeability: float32 [3, 256, 65536], P(None, 'gx', 'gy'), may hold values from 0.03 to 1000, as said below
Outputs:
- fine_pressure: float32 [256, 65536], P('gx', 'gy')
- twin_pressure: float32 [128, 16384], P('gx', 'gy')
Inputs may be any that keep to these rules, and one draw needn't show every extreme that they name: `permeability`: positive conductivities; entry 0, 1, 2 of the first dimension is the conductivity along the grid's first, second, third dimension.
All inputs are finite; a program needn't handle non-finite values.
Results may differ from a plain program's by a relative error of at most 0.0003.
Values sent between devices are 32-bit elements; how exact they have to be, the bound alone decides.
A program may use at most 192 MiB of HBM per device.

v0:
```python
import jax
import jax.numpy as jnp
from jax import lax
from jax.sharding import PartitionSpec as P

EL = 32
ELZ = 16
MX = 4
MZ = 2
EZ = 2
PATCH_ITERS = 3
COARSE_ITERS = 2


def shifted(shard, axis, by):
    count = lax.axis_size(axis)
    return lax.ppermute(shard, axis, [(i, (i + by) % count) for i in range(count)])


def padded_2(cells, sides, width):
    for axis, dim in sides:
        count = lax.axis_size(axis)
        head = lax.slice_in_dim(cells, 0, width, axis=dim)
        tail = lax.slice_in_dim(cells, cells.shape[dim] - width, cells.shape[dim], axis=dim)
        cells = jnp.concatenate(
            [
                lax.ppermute(tail, axis, [(i, (i + 1) % count) for i in range(count)]),
                cells,
                lax.ppermute(head, axis, [((i + 1) % count, i) for i in range(count)]),
            ],
            axis=dim,
        )
    return cells


def harmonic(first, second, spacing):
    return spacing * 2.0 * first * second / (first + second)


def face_weights(conduct, width, spacing):
    weight_rows = harmonic(conduct[0][..., :-width], conduct[0][..., width:], spacing)
    weight_cols = harmonic(conduct[1][..., :-1], conduct[1][..., 1:], spacing)
    column = jnp.arange(weight_cols.shape[-1], dtype=jnp.int32) % width
    weight_cols = jnp.where(column == width - 1, jnp.zeros_like(weight_cols), weight_cols)
    weight_depth = harmonic(conduct[2][:, :-1], conduct[2][:, 1:], spacing)
    return (weight_rows, weight_cols, weight_depth)


def apply_operator(field, weights, width):
    weight_rows, weight_cols, weight_depth = weights
    flux = weight_rows * (field[..., :-width] - field[..., width:])
    result = jnp.pad(flux, ((0, 0), (0, 0), (0, 0), (0, width))) - jnp.pad(
        flux, ((0, 0), (0, 0), (0, 0), (width, 0))
    )
    flux = weight_cols * (field[..., :-1] - field[..., 1:])
    result = (
        result
        + jnp.pad(flux, ((0, 0), (0, 0), (0, 0), (0, 1)))
        - jnp.pad(flux, ((0, 0), (0, 0), (0, 0), (1, 0)))
    )
    flux = weight_depth * (field[:, :, :-1] - field[:, :, 1:])
    result = (
        result
        + jnp.pad(flux, ((0, 0), (0, 0), (0, 1), (0, 0)))
        - jnp.pad(flux, ((0, 0), (0, 0), (1, 0), (0, 0)))
    )
    return result


def interior_mask(depth, rows, width):
    level = jnp.arange(depth, dtype=jnp.int32)[:, None]
    cell = jnp.arange(rows * width, dtype=jnp.int32)[None, :]
    row_index = cell // width
    line_index = cell % width
    inside = (
        (level > 0)
        & (level < depth - 1)
        & (row_index > 0)
        & (row_index < rows - 1)
        & (line_index > 0)
        & (line_index < width - 1)
    )
    return inside.astype(jnp.float32)


def shape_functions(depth, rows, width, edge, edge_depth, margin, margin_depth):
    cell = jnp.arange(rows * width, dtype=jnp.int32)
    place_rows = ((cell // width).astype(jnp.float32) - margin + 0.5) / edge
    place_cols = ((cell % width).astype(jnp.float32) - margin + 0.5) / edge
    place_depth = (
        jnp.arange(depth, dtype=jnp.int32).astype(jnp.float32) - margin_depth + 0.5
    ) / edge_depth
    factors = []
    for basis in range(8):
        along_rows = place_rows if basis // 4 else 1.0 - place_rows
        along_cols = place_cols if basis // 2 % 2 else 1.0 - place_cols
        along_depth = place_depth if basis % 2 else 1.0 - place_depth
        factors.append(along_depth[:, None] * (along_rows * along_cols)[None, :])
    return jnp.stack(factors)[:, None]


def patch_fields(block, edge_depth, margin_depth):
    depth = edge_depth + 2 * margin_depth
    count = (block.shape[3] - 2 * margin_depth) // edge_depth
    pieces = [
        block[:, :, :, index * edge_depth : index * edge_depth + depth] for index in range(count)
    ]
    stacked = jnp.stack(pieces, axis=1)
    return jnp.transpose(stacked, (0, 1, 4, 2, 3)).reshape(
        3, count, depth, block.shape[1] * block.shape[2]
    )


def solve_column(block, edge, edge_depth, margin, margin_depth, spacing):
    rows = block.shape[1]
    width = block.shape[2]
    depth = edge_depth + 2 * margin_depth
    conduct = patch_fields(block, edge_depth, margin_depth)
    count = conduct.shape[1]
    weights = face_weights(conduct, width, spacing)
    inside = interior_mask(depth, rows, width)
    start = shape_functions(depth, rows, width, edge, edge_depth, margin, margin_depth)
    residual = -inside * apply_operator(start, weights, width)
    direction = residual
    norm_now = jnp.sum(residual * residual, axis=(2, 3), keepdims=True)
    update = jnp.zeros_like(residual)
    for step in range(PATCH_ITERS):
        image = inside * apply_operator(direction, weights, width)
        alpha = norm_now / jnp.sum(direction * image, axis=(2, 3), keepdims=True)
        update = update + alpha * direction
        residual = residual - alpha * image
        norm_next = jnp.sum(residual * residual, axis=(2, 3), keepdims=True)
        direction = residual + norm_next / norm_now * direction
        norm_now = norm_next
    solution = start + update
    local = solution.reshape(8, count, depth, rows, width)[
        :,
        :,
        margin_depth : margin_depth + edge_depth,
        margin : margin + edge,
        margin : margin + edge,
    ]
    local = local.reshape(8, count, edge_depth, edge * edge)
    element_conduct = conduct.reshape(3, count, depth, rows, width)[
        :,
        :,
        margin_depth : margin_depth + edge_depth,
        margin : margin + edge,
        margin : margin + edge,
    ]
    element_conduct = element_conduct.reshape(3, count, edge_depth, edge * edge)
    inner_rows, inner_cols, inner_depth = face_weights(element_conduct, edge, spacing)
    jump = local[..., :-edge] - local[..., edge:]
    stiffness = jnp.einsum(
        "aezn,bezn->eab", jump * inner_rows, jump, precision=lax.Precision.HIGHEST
    )
    jump = local[..., :-1] - local[..., 1:]
    stiffness = stiffness + jnp.einsum(
        "aezn,bezn->eab", jump * inner_cols, jump, precision=lax.Precision.HIGHEST
    )
    jump = local[:, :, :-1] - local[:, :, 1:]
    stiffness = stiffness + jnp.einsum(
        "aezn,bezn->eab", jump * inner_depth, jump, precision=lax.Precision.HIGHEST
    )
    return (local, stiffness)


def coarsen(block):
    comps, rows, width, depth = block.shape
    grouped = block.reshape(comps, rows // 2, 2, width // 2, 2, depth // 2, 2)
    return 0.125 * jnp.sum(grouped, axis=(2, 4, 6))


def corner_stack(corner_first, corner_rows, corner_cols, corner_both, count):
    table = [[corner_first, corner_cols], [corner_rows, corner_both]]
    values = []
    for basis in range(8):
        lift = basis % 2
        values.append(table[basis // 4][basis // 2 % 2][..., lift : lift + count])
    return jnp.stack(values, axis=-1)


def spread(values):
    parts = [[None, None], [None, None]]
    for basis in range(8):
        lift = basis % 2
        widths = [(0, 0)] * (values.ndim - 2) + [(lift, 1 - lift)]
        padded = jnp.pad(values[..., basis], widths)
        first = basis // 4
        second = basis // 2 % 2
        if parts[first][second] is None:
            parts[first][second] = padded
        else:
            parts[first][second] = parts[first][second] + padded
    return parts


def pressure_tile(local, weights, edge):
    combined = jnp.sum(jnp.transpose(weights)[:, :, None, None] * local, axis=0)
    count = combined.shape[0]
    depth = combined.shape[1]
    return jnp.transpose(combined.reshape(count, depth, edge, edge), (2, 3, 0, 1)).reshape(
        edge, edge, count * depth
    )


def neighbours(nodes):
    next_rows = shifted(nodes, "gx", -1)
    fetched = shifted(jnp.stack([nodes[:, 0], next_rows[:, 0]]), "gy", -1)
    next_cols = jnp.concatenate([nodes[:, 1:], fetched[0][:, None]], axis=1)
    next_both = jnp.concatenate([next_rows[:, 1:], fetched[1][:, None]], axis=1)
    return (next_rows, next_cols, next_both)


def local_operator(stiffness, nodes, count):
    next_rows, next_cols, next_both = neighbours(nodes)
    element = corner_stack(nodes, next_rows, next_cols, next_both, count)
    local = jnp.einsum("lckab,lckb->lcka", stiffness, element, precision=lax.Precision.HIGHEST)
    parts = spread(local)
    col_part = parts[0][1]
    both_part = parts[1][1]
    returned = shifted(jnp.stack([col_part[:, -1], both_part[:, -1]]), "gy", 1)
    moved_cols = jnp.concatenate([returned[0][:, None], col_part[:, :-1]], axis=1)
    moved_both = jnp.concatenate([returned[1][:, None], both_part[:, :-1]], axis=1)
    across = shifted(parts[1][0] + moved_both, "gx", 1)
    return parts[0][0] + moved_cols + across


def squares(residual):
    return lax.psum(jnp.sum(residual * residual, axis=(1, 2), keepdims=True), ("gx", "gy"))


def spread_solve(stiffness, columns, count):
    level = jnp.arange(count + 1, dtype=jnp.int32)
    inside = ((level > 0) & (level < count)).astype(jnp.float32)
    boundary = jnp.broadcast_to((level == 0).astype(jnp.float32), (2, columns, count + 1))
    source = -inside * local_operator(stiffness, boundary, count)
    update = jnp.zeros_like(source)
    residual = source
    direction = source
    norm_now = squares(residual)
    for step in range(COARSE_ITERS):
        image = inside * local_operator(stiffness, direction, count)
        alpha = norm_now / lax.psum(
            jnp.sum(direction * image, axis=(1, 2), keepdims=True), ("gx", "gy")
        )
        update = update + alpha * direction
        residual = residual - alpha * image
        norm_next = squares(residual)
        direction = residual + norm_next / norm_now * direction
        norm_now = norm_next
    return boundary + update


def shards(permeability):
    depth_total = ELZ * EZ
    shaped = permeability.reshape(
        3, permeability.shape[1], permeability.shape[2] // depth_total, depth_total
    )
    rimmed = padded_2(shaped, (("gx", 1), ("gy", 2)), MX)
    half_edge = EL // 2
    columns = shaped.shape[2] // EL

    def column_work(offset):
        block = lax.dynamic_slice_in_dim(rimmed, offset, EL + 2 * MX, 2)
        fine_block = jnp.pad(block, ((0, 0), (0, 0), (0, 0), (MZ, MZ)), mode="edge")
        twin_block = coarsen(fine_block)
        fine_local, fine_stiff = solve_column(fine_block, EL, ELZ, MX, MZ, 1.0)
        twin_local, twin_stiff = solve_column(
            twin_block, half_edge, ELZ // 2, MX // 2, MZ // 2, 2.0
        )
        return (fine_local, fine_stiff, twin_local, twin_stiff)

    offsets = jnp.arange(columns, dtype=jnp.int32) * EL
    fine_local, fine_stiff, twin_local, twin_stiff = lax.map(column_work, offsets)
    stiffness = jnp.stack([fine_stiff, twin_stiff])
    count = stiffness.shape[2]
    corner_first = spread_solve(stiffness, columns, count)
    corner_rows, corner_cols, corner_both = neighbours(corner_first)
    weights = corner_stack(corner_first, corner_rows, corner_cols, corner_both, count)
    fine_tiles = [
        pressure_tile(fine_local[column], weights[0, column], EL) for column in range(columns)
    ]
    twin_tiles = [
        pressure_tile(twin_local[column], weights[1, column], half_edge)
        for column in range(columns)
    ]
    fine_pressure = jnp.concatenate(fine_tiles, axis=1)
    twin_pressure = jnp.concatenate(twin_tiles, axis=1)
    return (fine_pressure.reshape(EL, -1), twin_pressure.reshape(half_edge, -1))


def solution(mesh):
    placed = (P(None, "gx", "gy"),)
    return jax.shard_map(
        shards,
        mesh=mesh,
        in_specs=placed,
        out_specs=(P("gx", "gy"), P("gx", "gy")),
        check_vma=False,
    )
```

profile of v0, /device:TPU:1, one launch (start us, length us, event | category | flops | bytes accessed | tf_op | source)
XLA Modules:
  0.0 635.2 jit_solution(149568154038995864)
XLA Ops:
  6.1 3.9 collective-permute-start.1
  13.8 4.4 collective-permute-done.4
  39.7 4.5 pad_maximum_fusion.3
  44.2 299.3 %while.21 = (s32[]{:T(128)}, f32[2,8,2,16,1024]{4,1,3,2,0:T(8,128)}, f32[2,2,8,8]{3,2,1,0:T(8,128)}, f32[2,8,2,8,256]{4,1,3,2,0:T(8,128)}, f32[2,2,8,8]{3,2,1,0:...) while((s32[]{:T(128)}, ...), condition=%wide.region_14.15_spmd, body=%wide.region_0.14_spmd.sunk | while | flops 130577320 | bytes 255059728 | solution.py:275
  90.3 5.9 reshape.1503
  96.2 5.7 slice.2293
  102.0 3.7 broadcast_in_dim.249
  106.8 3.9 reshape.1504
  131.4 26.2 %reshape.1505 = f32[3,20,2,20,2,18,2]{4,3,2,1,6,5,0:T(8,128)} reshape(f32[3,40,40,36]{2,1,3,0:T(8,128)} %pad_maximum_fusion.26) | data formatting | bytes 1382400 | tf_op jit(solution)/shard_map/while/body/eval_jaxpr/reshape | solution.py:170
  157.7 19.5 %reduce_sum.329 = f32[3,20,20,18]{2,1,3,0:T(8,128)S(1)} reduce(f32[3,20,2,20,2,18,2]{4,3,2,1,6,5,0:T(8,128)} %reshape.1505, f32[]{:T(128)} %constant.340.clone.31..sunk), dimensions={2,4,6}, to_apply=%region_7.7 | reduce | flops 151200 | bytes 777604 | tf_op jit(solution)/shard_map/while/body/eval_jaxpr/reduce_sum | solution.py:171
  235.5 5.9 reshape.1503
  241.5 5.7 slice.2293
  247.2 3.7 broadcast_in_dim.249
  252.0 4.0 reshape.1504
  271.7 3.0 fusion.264
  276.7 26.2 %reshape.1505 = f32[3,20,2,20,2,18,2]{4,3,2,1,6,5,0:T(8,128)} reshape(f32[3,40,40,36]{2,1,3,0:T(8,128)} %pad_maximum_fusion.26) | data formatting | bytes 1382400 | tf_op jit(solution)/shard_map/while/body/eval_jaxpr/reshape | solution.py:170
  302.9 19.7 %reduce_sum.329 = f32[3,20,20,18]{2,1,3,0:T(8,128)S(1)} reduce(f32[3,20,2,20,2,18,2]{4,3,2,1,6,5,0:T(8,128)} %reshape.1505, f32[]{:T(128)} %constant.340.clone.31..sunk), dimensions={2,4,6}, to_apply=%region_7.7 | reduce | flops 151200 | bytes 777604 | tf_op jit(solution)/shard_map/while/body/eval_jaxpr/reduce_sum | solution.py:171
  344.9 7.2 %collective-permute-done.6 = f32[2,2,3]{2,1,0:T(2,128)S(1)} collective-permute-done((f32[2,2,3]{2,1,0:T(2,128)S(1)}, f32[2,2,3]{2,1,0:T(2,128)S(1)}, u32[]{:S(2)}, u32[]{:S(2)}) %collective-permute-start.6) | collective-permute-done | bytes 80 | tf_op jit(solution)/shard_map/ppermute | solution.py:17
  352.2 4.6 collective-permute-done.7
  360.1 7.4 %collective-permute-start.9 = (f32[2,2,3]{2,1,0:T(2,128)S(1)}, f32[2,2,3]{2,1,0:T(2,128)S(1)}, u32[]{:S(2)}, u32[]{:S(2)}) collective-permute-start(f32[2,2,3]{2,1,0:T(2,128)S(1)} %pad_maximum_fusion.20), channel_id=1, source_target_pairs={{0,31},{1,0},{2,1},{3,2},{4,3},{5,4},{6,5},{7,6},{8,7},{9,8},{10,9... | collective-permute-start | bytes 152 | tf_op jit(solution)/shard_map/ppermute | solution.py:17
  371.6 4.2 collective-permute-done.11
  376.6 77.9 %all-reduce.72 = (f32[2,1,1]{0,2,1:T(1,128)S(1)}, f32[2,1,1]{0,2,1:T(1,128)S(1)}) all-reduce(f32[2,1,1]{0,2,1:T(1,128)S(1)} %bitcast.449, f32[2,1,1]{0,2,1:T(1,128)S(1)} %bitcast.448), channel_id=1, replica_groups=mesh['gx'=8,'gy'=32] {'gx','gy'}, use_global_device_ids=true, to_apply=%region_16.17 | all-reduce | flops 4 | bytes 32 | tf_op jit(solution)/shard_map/psum | solution.py:230
  454.7 73.6 %psum.30 = f32[2,1,1]{0,2,1:T(1,128)S(1)} all-reduce(f32[2,1,1]{0,2,1:T(1,128)S(1)} %bitcast.451), channel_id=1, replica_groups=mesh['gx'=8,'gy'=32] {'gx','gy'}, use_global_device_ids=true, to_apply=%region_20.21 | all-reduce | flops 2 | bytes 16 | tf_op jit(solution)/shard_map/psum | solution.py:230
  543.3 77.1 %psum.31 = f32[2,1,1]{0,2,1:T(1,128)S(1)} all-reduce(f32[2,1,1]{0,2,1:T(1,128)S(1)} %bitcast.450), channel_id=1, replica_groups=mesh['gx'=8,'gy'=32] {'gx','gy'}, use_global_device_ids=true, to_apply=%region_22.23 | all-reduce | flops 2 | bytes 16 | tf_op jit(solution)/shard_map/psum | solution.py:244
  (559 shorter events, 220.7 us)
Async XLA Ops:
  3.7 20.6 %collective-permute-start = (f32[3,4,64,32]{3,2,1,0:T(8,128)}, f32[3,4,64,32]{3,2,1,0:T(8,128)}, u32[]{:S(2)}, u32[]{:S(2)}) collective-permute-start(f32[3,4,64,32]{3,2,1,0:T(8,128)} %get-tuple-element.370), channel_id=1, source_target_pairs={{0,32},{32,64},{64,96},{96,128},{128,160},{160,192},{192,224},{224... | collective-permute-start | bytes 294920 | tf_op jit(solution)/shard_map/ppermute | solution.py:27
  6.1 19.5 %collective-permute-start.1 = (f32[3,4,64,32]{3,2,1,0:T(8,128)}, f32[3,4,64,32]{3,2,1,0:T(8,128)S(1)}, u32[]{:S(2)}, u32[]{:S(2)}) collective-permute-start(f32[3,4,64,32]{3,2,1,0:T(8,128)} %get-tuple-element.369), channel_id=1, source_target_pairs={{32,0},{64,32},{96,64},{128,96},{160,128},{192,160},{224,192},{0,2... | collective-permute-start | bytes 294920 | tf_op jit(solution)/shard_map/ppermute | solution.py:29
  10.1 20.1 %copy-start.18 = (f32[3]{0:T(128)}, f32[3]{0:T(128)S(1)}, u32[]{:S(2)}) copy-start(f32[3]{0:T(128)S(1)} %compare_convert_fusion) | copy-start | bytes 40
  10.1 8.1 %collective-permute-start.4 = (f32[2,2,3]{2,0,1:T(2,128)S(1)}, f32[2,2,3]{2,0,1:T(2,128)S(1)}, u32[]{:S(2)}, u32[]{:S(2)}) collective-permute-start(f32[2,2,3]{2,0,1:T(2,128)S(1)} %broadcast_in_dim.227), channel_id=1, source_target_pairs={{0,224},{32,0},{64,32},{96,64},{128,96},{160,128},{192,160},{224,1... | collective-permute-start | bytes 152 | tf_op jit(solution)/shard_map/ppermute | solution.py:17
  19.3 4.3 collective-permute-start.5
  25.4 4.9 copy-start.19
  27.6 7.9 %collective-permute-start.3 = (f32[3,40,4,32]{3,2,1,0:T(4,128)S(1)}, f32[3,40,4,32]{3,2,1,0:T(4,128)S(1)}, u32[]{:S(2)}, u32[]{:S(2)}) collective-permute-start(f32[3,40,4,32]{3,2,1,0:T(4,128)S(1)} %get-tuple-element.368), channel_id=1, source_target_pairs={{1,0},{2,1},{3,2},{4,3},{5,4},{6,5},{7,6},{8,7},{9,8},{10,9},{11,1... | collective-permute-start | bytes 184328 | tf_op jit(solution)/shard_map/ppermute | solution.py:29
  30.2 7.4 %collective-permute-start.2 = (f32[3,40,4,32]{3,2,1,0:T(4,128)S(1)}, f32[3,40,4,32]{3,2,1,0:T(4,128)S(1)}, u32[]{:S(2)}, u32[]{:S(2)}) collective-permute-start(f32[3,40,4,32]{3,2,1,0:T(4,128)S(1)} %get-tuple-element.367), channel_id=1, source_target_pairs={{0,1},{1,2},{2,3},{3,4},{4,5},{5,6},{6,7},{7,8},{8,9},{9,10},{10,1... | collective-permute-start | bytes 184328 | tf_op jit(solution)/shard_map/ppermute | solution.py:27
  125.3 4.6 copy-start.9
  125.3 4.6 copy-start.11
  270.5 4.6 copy-start.9
  270.5 4.6 copy-start.11
  344.8 7.3 %collective-permute-start.6 = (f32[2,2,3]{2,1,0:T(2,128)S(1)}, f32[2,2,3]{2,1,0:T(2,128)S(1)}, u32[]{:S(2)}, u32[]{:S(2)}) collective-permute-start(f32[2,2,3]{2,1,0:T(2,128)S(1)} %pad_maximum_fusion.19), channel_id=1, source_target_pairs={{0,1},{1,2},{2,3},{3,4},{4,5},{5,6},{6,7},{7,8},{8,9},{9,10},{10,1... | collective-permute-start | bytes 152 | tf_op jit(solution)/shard_map/ppermute | solution.py:17
  352.2 4.6 collective-permute-start.7
  357.6 2.4 collective-permute-start.8
  360.1 8.2 %collective-permute-start.9 = (f32[2,2,3]{2,1,0:T(2,128)S(1)}, f32[2,2,3]{2,1,0:T(2,128)S(1)}, u32[]{:S(2)}, u32[]{:S(2)}) collective-permute-start(f32[2,2,3]{2,1,0:T(2,128)S(1)} %pad_maximum_fusion.20), channel_id=1, source_target_pairs={{0,31},{1,0},{2,1},{3,2},{4,3},{5,4},{6,5},{7,6},{8,7},{9,8},{10,9... | collective-permute-start | bytes 152 | tf_op jit(solution)/shard_map/ppermute | solution.py:17
  370.2 1.2 collective-permute-start.10
  371.5 4.2 collective-permute-start.11
  528.5 2.7 collective-permute-start.12
  531.2 3.9 collective-permute-start.13
  537.0 1.2 collective-permute-start.14
  538.3 4.2 collective-permute-start.15
  621.2 2.7 collective-permute-start.16
  623.9 3.7 collective-permute-start.17
  (33 other events, 62.1 us)
where the time goes:
time: 646 us; the launch traced here: 635 us
  blocking collectives  229 us (35%)
  local copies, waits for them, and re-layouts  188 us (29%)
  other arithmetic  118 us (18%)
  waiting for transfers between devices  34.7 us (5%)
  starting transfers between devices  28.8 us (4%)
  matrix products  20.8 us (3%)
  loops' own time  14.6 us (2%)
    psum x2, blocking collectives, squares(): lax.psum(jnp.sum(residual * residual, axis=(1, 2), keepdims=True), ('gx',...  152 us
    psum x1, blocking collectives, spread_solve(): lax.psum(jnp.sum(direction * image, axis=(1, 2), keepdims=True), ('gx', '...  77.1 us
    reshape x2, local copies, waits for them, and re-layouts, coarsen(): grouped = block.reshape(comps, rows // 2, 2, width // 2, 2, depth // 2, 2)  52.5 us
    reduce_sum x2, other arithmetic, coarsen(): return 0.125 * jnp.sum(grouped, axis=(2, 4, 6))  39.3 us
    ppermute x14, waiting for transfers between devices, shifted(): lax.ppermute(shard, axis, [(i, (i + by) % count) for i in range(count)])  34.7 us
    ppermute x14, starting transfers between devices, shifted(): lax.ppermute(shard, axis, [(i, (i + by) % count) for i in range(count)])  19.8 us
    reshape x4, local copies, waits for them, and re-layouts, solve_column(): solution.reshape(8, count, depth, rows, width)  15.7 us
    slice x4, local copies, waits for them, and re-layouts, solve_column(): solution.reshape(8, count, depth, rows, width)  15 us
  transfers between devices with their start and end apart: 18, of which 14 were waited for; matrix products, arithmetic and copies ran while one was open for 2% of the time, Pallas kernels for 0%

commit v1 on v0

--- a/solution.py
+++ b/solution.py
@@ -10,6 +10,12 @@
 EZ = 2
 PATCH_ITERS = 3
 COARSE_ITERS = 2
+
+
+def gather_and_add(array, axis):
+    pieces = lax.all_gather(array, axis, axis=0, tiled=False)
+    total = pieces.sum(axis=0)
+    return total
 
 
 def shifted(shard, axis, by):
@@ -241,7 +247,7 @@
     norm_now = squares(residual)
     for step in range(COARSE_ITERS):
         image = inside * local_operator(stiffness, direction, count)
-        alpha = norm_now / lax.psum(
+        alpha = norm_now / gather_and_add(
             jnp.sum(direction * image, axis=(1, 2), keepdims=True), ("gx", "gy")
         )
         update = update + alpha * direction

time: 646 us -> 646 us (level)
    unnamed x0 -> x1, blocking collectives: none -> 77.3 us
    psum x1 -> x0, blocking collectives: 77.1 us -> none  [spread_solve(): lax.psum(jnp.sum(direction * image, axis=(1, 2), keepdims=True), ('gx', '...]
where the time goes in v1:
time: 646 us; the launch traced here: 635 us
  blocking collectives  229 us (35%)
  local copies, waits for them, and re-layouts  188 us (29%)
  other arithmetic  119 us (18%)
  waiting for transfers between devices  34.4 us (5%)
  starting transfers between devices  28.7 us (4%)
  matrix products  20.8 us (3%)
  loops' own time  14.1 us (2%)
    psum x2, blocking collectives, squares(): lax.psum(jnp.sum(residual * residual, axis=(1, 2), keepdims=True), ('gx',...  151 us
    unnamed x1, blocking collectives  77.3 us
    reshape x2, local copies, waits for them, and re-layouts, coarsen(): grouped = block.reshape(comps, rows // 2, 2, width // 2, 2, depth // 2, 2)  52.3 us
    reduce_sum x2, other arithmetic, coarsen(): return 0.125 * jnp.sum(grouped, axis=(2, 4, 6))  39.3 us
    ppermute x14, waiting for transfers between devices, shifted(): lax.ppermute(shard, axis, [(i, (i + by) % count) for i in range(count)])  34.4 us
    ppermute x14, starting transfers between devices, shifted(): lax.ppermute(shard, axis, [(i, (i + by) % count) for i in range(count)])  19.6 us
    reshape x4, local copies, waits for them, and re-layouts, solve_column(): solution.reshape(8, count, depth, rows, width)  15.6 us
    slice x4, local copies, waits for them, and re-layouts, solve_column(): solution.reshape(8, count, depth, rows, width)  15 us
  transfers between devices with their start and end apart: 18, of which 14 were waited for; matrix products, arithmetic and copies ran while one was open for 2% of the time, Pallas kernels for 0%

profile of v1, /device:TPU:1, one launch (start us, length us, event | category | flops | bytes accessed | tf_op | source)
XLA Modules:
  0.0 635.0 jit_solution(5073341999664808553)
XLA Ops:
  6.1 3.9 collective-permute-start.1
  13.7 4.5 collective-permute-done.4
  39.6 4.5 pad_maximum_fusion.3
  44.1 298.6 %while.21 = (s32[]{:T(128)}, f32[2,8,2,16,1024]{4,1,3,2,0:T(8,128)}, f32[2,2,8,8]{3,2,1,0:T(8,128)}, f32[2,8,2,8,256]{4,1,3,2,0:T(8,128)}, f32[2,2,8,8]{3,2,1,0:...) while((s32[]{:T(128)}, ...), condition=%wide.region_14.15_spmd, body=%wide.region_0.14_spmd.sunk | while | flops 130577320 | bytes 255059728 | solution.py:281
  90.2 5.9 reshape.1513
  96.1 5.7 slice.2293
  101.8 3.7 broadcast_in_dim.241
  106.6 3.9 reshape.1514
  126.3 3.0 fusion.266
  131.3 26.2 %reshape.1515 = f32[3,20,2,20,2,18,2]{4,3,2,1,6,5,0:T(8,128)} reshape(f32[3,40,40,36]{2,1,3,0:T(8,128)} %pad_maximum_fusion.26) | data formatting | bytes 1382400 | tf_op jit(solution)/shard_map/while/body/eval_jaxpr/reshape | solution.py:176
  157.5 19.5 %reduce_sum.355 = f32[3,20,20,18]{2,1,3,0:T(8,128)S(1)} reduce(f32[3,20,2,20,2,18,2]{4,3,2,1,6,5,0:T(8,128)} %reshape.1515, f32[]{:T(128)} %constant.353.clone.1..sunk), dimensions={2,4,6}, to_apply=%region_7.7 | reduce | flops 151200 | bytes 777604 | tf_op jit(solution)/shard_map/while/body/eval_jaxpr/reduce_sum | solution.py:177
  235.4 5.9 reshape.1513
  241.3 5.7 slice.2293
  247.0 3.7 broadcast_in_dim.241
  251.8 4.0 reshape.1514
  276.5 26.2 %reshape.1515 = f32[3,20,2,20,2,18,2]{4,3,2,1,6,5,0:T(8,128)} reshape(f32[3,40,40,36]{2,1,3,0:T(8,128)} %pad_maximum_fusion.26) | data formatting | bytes 1382400 | tf_op jit(solution)/shard_map/while/body/eval_jaxpr/reshape | solution.py:176
  302.7 19.7 %reduce_sum.355 = f32[3,20,20,18]{2,1,3,0:T(8,128)S(1)} reduce(f32[3,20,2,20,2,18,2]{4,3,2,1,6,5,0:T(8,128)} %reshape.1515, f32[]{:T(128)} %constant.353.clone.1..sunk), dimensions={2,4,6}, to_apply=%region_7.7 | reduce | flops 151200 | bytes 777604 | tf_op jit(solution)/shard_map/while/body/eval_jaxpr/reduce_sum | solution.py:177
  344.1 7.1 %collective-permute-done.6 = f32[2,2,3]{2,1,0:T(2,128)S(1)} collective-permute-done((f32[2,2,3]{2,1,0:T(2,128)S(1)}, f32[2,2,3]{2,1,0:T(2,128)S(1)}, u32[]{:S(2)}, u32[]{:S(2)}) %collective-permute-start.6) | collective-permute-done | bytes 80 | tf_op jit(solution)/shard_map/ppermute | solution.py:23
  351.3 4.6 collective-permute-done.7
  359.1 7.4 %collective-permute-start.9 = (f32[2,2,3]{2,1,0:T(2,128)S(1)}, f32[2,2,3]{2,1,0:T(2,128)S(1)}, u32[]{:S(2)}, u32[]{:S(2)}) collective-permute-start(f32[2,2,3]{2,1,0:T(2,128)S(1)} %pad_maximum_fusion.20), channel_id=1, source_target_pairs={{0,31},{1,0},{2,1},{3,2},{4,3},{5,4},{6,5},{7,6},{8,7},{9,8},{10,9... | collective-permute-start | bytes 152 | tf_op jit(solution)/shard_map/ppermute | solution.py:23
  370.6 4.2 collective-permute-done.11
  375.9 77.9 %all-reduce.74 = (f32[2,1,1]{0,2,1:T(1,128)S(1)}, f32[512]{0:T(512)S(1)}) all-reduce(f32[2,1,1]{0,2,1:T(1,128)S(1)} %bitcast.454, f32[512]{0:T(512)S(1)} %dynamic-update-slice), channel_id=1, replica_groups=mesh['gx'=8,'gy'=32] {'gx','gy'}, use_global_device_ids=true, to_apply=%region_16.17 | all-reduce | flops 514 | bytes 4112 | tf_op jit(solution)/shard_map/psum | solution.py:236
  454.2 73.6 %psum.15 = f32[2,1,1]{0,2,1:T(1,128)S(1)} all-reduce(f32[2,1,1]{0,2,1:T(1,128)S(1)} %bitcast.455), channel_id=1, replica_groups=mesh['gx'=8,'gy'=32] {'gx','gy'}, use_global_device_ids=true, to_apply=%region_20.21 | all-reduce | flops 2 | bytes 16 | tf_op jit(solution)/shard_map/psum | solution.py:236
  542.9 77.3 %all-reduce.73 = f32[512]{0:T(512)S(1)} all-reduce(f32[512]{0:T(512)S(1)} %dynamic-update-slice.1), channel_id=3, replica_groups=mesh['gx'=8,'gy'=32] {'gx','gy'}, use_global_device_ids=true, to_apply=%add.73 | all-reduce | flops 512 | bytes 4096
  (567 shorter events, 221.1 us)
Async XLA Ops:
  3.7 20.4 %collective-permute-start = (f32[3,4,64,32]{3,2,1,0:T(8,128)}, f32[3,4,64,32]{3,2,1,0:T(8,128)}, u32[]{:S(2)}, u32[]{:S(2)}) collective-permute-start(f32[3,4,64,32]{3,2,1,0:T(8,128)} %get-tuple-element.370), channel_id=1, source_target_pairs={{0,32},{32,64},{64,96},{96,128},{128,160},{160,192},{192,224},{224... | collective-permute-start | bytes 294920 | tf_op jit(solution)/shard_map/ppermute | solution.py:33
  6.1 19.2 %collective-permute-start.1 = (f32[3,4,64,32]{3,2,1,0:T(8,128)}, f32[3,4,64,32]{3,2,1,0:T(8,128)S(1)}, u32[]{:S(2)}, u32[]{:S(2)}) collective-permute-start(f32[3,4,64,32]{3,2,1,0:T(8,128)} %get-tuple-element.369), channel_id=1, source_target_pairs={{32,0},{64,32},{96,64},{128,96},{160,128},{192,160},{224,192},{0,2... | collective-permute-start | bytes 294920 | tf_op jit(solution)/shard_map/ppermute | solution.py:35
  10.1 20.0 %copy-start.18 = (f32[3]{0:T(128)}, f32[3]{0:T(128)S(1)}, u32[]{:S(2)}) copy-start(f32[3]{0:T(128)S(1)} %compare_convert_fusion) | copy-start | bytes 40
  10.1 8.1 %collective-permute-start.4 = (f32[2,2,3]{2,0,1:T(2,128)S(1)}, f32[2,2,3]{2,0,1:T(2,128)S(1)}, u32[]{:S(2)}, u32[]{:S(2)}) collective-permute-start(f32[2,2,3]{2,0,1:T(2,128)S(1)} %broadcast_in_dim.221), channel_id=1, source_target_pairs={{0,224},{32,0},{64,32},{96,64},{128,96},{160,128},{192,160},{224,1... | collective-permute-start | bytes 152 | tf_op jit(solution)/shard_map/ppermute | solution.py:23
  19.3 4.2 collective-permute-start.5
  25.1 5.0 copy-start.19
  27.4 8.1 %collective-permute-start.3 = (f32[3,40,4,32]{3,2,1,0:T(4,128)S(1)}, f32[3,40,4,32]{3,2,1,0:T(4,128)S(1)}, u32[]{:S(2)}, u32[]{:S(2)}) collective-permute-start(f32[3,40,4,32]{3,2,1,0:T(4,128)S(1)} %get-tuple-element.368), channel_id=1, source_target_pairs={{1,0},{2,1},{3,2},{4,3},{5,4},{6,5},{7,6},{8,7},{9,8},{10,9},{11,1... | collective-permute-start | bytes 184328 | tf_op jit(solution)/shard_map/ppermute | solution.py:35
  30.1 7.4 %collective-permute-start.2 = (f32[3,40,4,32]{3,2,1,0:T(4,128)S(1)}, f32[3,40,4,32]{3,2,1,0:T(4,128)S(1)}, u32[]{:S(2)}, u32[]{:S(2)}) collective-permute-start(f32[3,40,4,32]{3,2,1,0:T(4,128)S(1)} %get-tuple-element.367), channel_id=1, source_target_pairs={{0,1},{1,2},{2,3},{3,4},{4,5},{5,6},{6,7},{7,8},{8,9},{9,10},{10,1... | collective-permute-start | bytes 184328 | tf_op jit(solution)/shard_map/ppermute | solution.py:33
  125.1 4.6 copy-start.9
  125.1 4.6 copy-start.11
  270.3 4.6 copy-start.9
  270.3 4.6 copy-start.11
  344.0 7.2 %collective-permute-start.6 = (f32[2,2,3]{2,1,0:T(2,128)S(1)}, f32[2,2,3]{2,1,0:T(2,128)S(1)}, u32[]{:S(2)}, u32[]{:S(2)}) collective-permute-start(f32[2,2,3]{2,1,0:T(2,128)S(1)} %pad_maximum_fusion.19), channel_id=1, source_target_pairs={{0,1},{1,2},{2,3},{3,4},{4,5},{5,6},{6,7},{7,8},{8,9},{9,10},{10,1... | collective-permute-start | bytes 152 | tf_op jit(solution)/shard_map/ppermute | solution.py:23
  351.3 4.6 collective-permute-start.7
  356.7 2.4 collective-permute-start.8
  359.1 8.2 %collective-permute-start.9 = (f32[2,2,3]{2,1,0:T(2,128)S(1)}, f32[2,2,3]{2,1,0:T(2,128)S(1)}, u32[]{:S(2)}, u32[]{:S(2)}) collective-permute-start(f32[2,2,3]{2,1,0:T(2,128)S(1)} %pad_maximum_fusion.20), channel_id=1, source_target_pairs={{0,31},{1,0},{2,1},{3,2},{4,3},{5,4},{6,5},{7,6},{8,7},{9,8},{10,9... | collective-permute-start | bytes 152 | tf_op jit(solution)/shard_map/ppermute | solution.py:23
  369.3 1.2 collective-permute-start.10
  370.6 4.2 collective-permute-start.11
  527.9 2.7 collective-permute-start.12
  530.6 3.9 collective-permute-start.13
  536.4 1.2 collective-permute-start.14
  537.7 4.2 collective-permute-start.15
  621.3 2.4 collective-permute-start.16
  623.7 3.7 collective-permute-start.17
  (33 other events, 62.1 us)
